TPU v7x, 512 devices: a whole 4x4x16 slice. The times are simulated.
512 devices in a mesh: dp: 32 (over z, core), mp: 16 (over x, y).
Axes of the slice: x: 4, y: 4, z: 16, core: 2. Of those that a mesh axis runs over, the one named last changes fastest.
Arguments:
- hidden_in: bfloat16 [64, 512, 8192], P('dp', None, 'mp'), may hold values from -6 to 6
- query_act: bfloat16 [64, 512, 8192], P('dp', None, 'mp'), may hold values from -6 to 6
- key_act: bfloat16 [64, 512, 1024], P('dp'), may hold values from -6 to 6
- value_act: bfloat16 [64, 512, 1024], P('dp'), may hold values from -6 to 6
- ctx_grad: bfloat16 [64, 512, 8192], P('dp', None, 'mp'), may hold values from -6 to 6
- segment_ids: int32 [64, 512], P('dp'), may hold values from 0 to 3, never falling along the last dimension, each value on 1 to 256 neighbouring positions
- down_query: bfloat16 [8192, 128], P('mp'), may hold values from -0.0625 to 0.0625
- up_query: bfloat16 [128, 8192], P(None, 'mp'), may hold values from -0.5 to 0.5
- down_value: bfloat16 [8192, 128], P('mp'), may hold values from -0.0625 to 0.0625
- up_value: bfloat16 [128, 1024], replicated, may hold values from -0.5 to 0.5
- block_rows: int32 [3, 8192], P(None, 'mp'), may hold values from 0 to 63
- tile_rows: int32 [3, 8192], P(None, 'mp'), may hold values from 0 to 7
- block_value: int32 [1024], replicated, may hold values from 0 to 63
- tile_value: int32 [1024], replicated, may hold values from 0 to 7
- tile_bank: bfloat16 [8, 128, 128], replicated, may hold values from -0.5 to 0.5
- seed_feats: bfloat16 [1024, 8192], P('dp', 'mp'), may hold values from -6 to 6
Outputs:
- scores: float32 [64, 1024], P('dp', 'mp')
All inputs are finite; a program needn't handle non-finite values.
Results may differ from a plain program's by a relative error of at most 0.022.
Values may be sent and summed in bfloat16 or wider, within the bound.
No kernel may reach another device: no remote copies, remote signals or barrier semaphores. Data moves between devices by JAX's collectives and lax.ppermute only.
A program may use at most 64 MiB of HBM per device.

v0:
```python
import math
import jax
import jax.numpy as jnp
from jax import lax
from jax.sharding import PartitionSpec as P

H = 64
KVH = 8
DH = 128
R = 128
K = 8192
PB = 128
NT = 8
EPS = 1e-06


def local(
    hidden_in,
    query_act,
    key_act,
    value_act,
    ctx_grad,
    segment_ids,
    down_query,
    up_query,
    down_value,
    up_value,
    block_rows,
    tile_rows,
    block_value,
    tile_value,
    tile_bank,
    seed_feats,
):
    model_index = lax.axis_index("mp")
    cand_count, seq_len, width_dev = query_act.shape
    heads_dev = width_dev // DH
    head_group = H // KVH
    kv_count = max(heads_dev // head_group, 1)
    repeats = heads_dev // kv_count
    kv_first = model_index * heads_dev // head_group
    kv_width = kv_count * DH
    key_local = lax.dynamic_slice_in_dim(key_act, kv_first * DH, kv_width, 2)
    value_local = lax.dynamic_slice_in_dim(value_act, kv_first * DH, kv_width, 2)
    up_local = lax.dynamic_slice_in_dim(up_value, kv_first * DH, kv_width, 1)
    block_local = lax.dynamic_slice_in_dim(block_value, kv_first * DH, kv_width, 0)
    tile_local = lax.dynamic_slice_in_dim(tile_value, kv_first * DH, kv_width, 0)

    def spread_heads(packed):
        five = packed.reshape(cand_count, seq_len, kv_count, 1, DH)
        return jnp.broadcast_to(five, (cand_count, seq_len, kv_count, repeats, DH)).reshape(
            cand_count, seq_len, heads_dev, DH
        )

    queries = query_act.reshape(cand_count, seq_len, heads_dev, DH)
    key_heads = spread_heads(key_local)
    value_heads = spread_heads(value_local)
    grad_heads = ctx_grad.reshape(cand_count, seq_len, heads_dev, DH)
    both_down = jnp.concatenate([down_query, down_value], axis=1)
    lowrank_part = jnp.einsum(
        "bsd,dr->bsr", hidden_in, both_down, preferred_element_type=jnp.float32
    )
    position = jnp.arange(seq_len, dtype=jnp.int32)
    allowed = (position[None, :] <= position[:, None])[None] & (
        segment_ids[:, :, None] == segment_ids[:, None, :]
    )
    score_scale = 1.0 / math.sqrt(DH)
    logits = (
        jnp.einsum("bqhd,bkhd->bhqk", queries, key_heads, preferred_element_type=jnp.float32)
        * score_scale
    )
    logits = jnp.where(allowed[:, None], logits, -1e30)
    row_top = jnp.max(logits, axis=-1, keepdims=True)
    exp_terms = jnp.exp(logits - row_top)
    attn_probs = exp_terms / jnp.sum(exp_terms, axis=-1, keepdims=True)
    value_grad = jnp.einsum(
        "bhqk,bqhd->bkhd",
        attn_probs.astype(jnp.bfloat16),
        grad_heads,
        preferred_element_type=jnp.float32,
    ).astype(jnp.bfloat16)
    prob_grad = jnp.einsum(
        "bqhd,bkhd->bhqk", grad_heads, value_heads, preferred_element_type=jnp.float32
    )
    row_delta = jnp.sum(attn_probs * prob_grad, axis=-1, keepdims=True)
    logit_grad = (attn_probs * (prob_grad - row_delta)).astype(jnp.bfloat16)
    query_grad = (
        jnp.einsum("bhqk,bkhd->bqhd", logit_grad, key_heads, preferred_element_type=jnp.float32)
        * score_scale
    )
    query_grad = query_grad.astype(jnp.bfloat16).reshape(cand_count, seq_len, width_dev)
    value_five = value_grad.reshape(cand_count, seq_len, kv_count, repeats, DH)
    up_three = up_local.reshape(R, kv_count, DH)
    back_query = jnp.einsum("bsc,rc->bsr", query_grad, up_query, preferred_element_type=jnp.float32)
    back_value = jnp.einsum(
        "bskgd,rkd->bsr", value_five, up_three, preferred_element_type=jnp.float32
    )
    back_part = jnp.concatenate([back_query, back_value], axis=2)
    lowrank_in, lowrank_back = lax.psum((lowrank_part, back_part), "mp")
    lowrank_in = lowrank_in.astype(jnp.bfloat16)
    lowrank_back = lowrank_back.astype(jnp.bfloat16)
    grad_down = jnp.einsum(
        "bsd,bsr->bdr", hidden_in, lowrank_back, preferred_element_type=jnp.float32
    )
    grad_upq = jnp.einsum(
        "bsr,bsc->bcr", lowrank_in[:, :, :R], query_grad, preferred_element_type=jnp.float32
    )
    grad_upv = jnp.einsum(
        "bsr,bskgd->bkdr", lowrank_in[:, :, R:], value_five, preferred_element_type=jnp.float32
    )
    grad_upv = grad_upv.reshape(cand_count, kv_width, R)
    grad_rows = jnp.concatenate(
        [grad_down[:, :, :R], grad_down[:, :, R:], grad_upq, grad_upv], axis=1
    )
    bucket_ids = jnp.concatenate(
        [(block_rows * NT + tile_rows).reshape(-1), block_local * NT + tile_local]
    )
    out_blocks = K // PB
    block_sums = jax.ops.segment_sum(
        jnp.moveaxis(grad_rows, 1, 0), bucket_ids, num_segments=out_blocks * NT
    )
    block_sums = (
        block_sums.reshape(out_blocks, NT, cand_count, R)
        .transpose(2, 0, 1, 3)
        .reshape(cand_count, out_blocks, NT * R)
    )
    tile_table = tile_bank.astype(jnp.float32).reshape(NT * R, PB)
    projected = jnp.einsum(
        "bkj,jp->bkp", block_sums, tile_table, precision=lax.Precision.HIGHEST
    ).reshape(cand_count, K)
    feat_slice = lax.psum_scatter(
        projected.astype(jnp.bfloat16), "mp", scatter_dimension=1, tiled=True
    ).astype(jnp.float32)
    feat_square = jnp.sum(feat_slice * feat_slice, axis=1)
    feat_half = feat_slice.astype(jnp.bfloat16)
    partial_value = jnp.einsum(
        "bk,sk->bs",
        feat_half,
        lax.all_gather(seed_feats, "dp", axis=0, tiled=True),
        preferred_element_type=jnp.float32,
    )
    total_square = lax.psum(feat_square, "mp")
    numerator = lax.psum_scatter(partial_value, "mp", scatter_dimension=1, tiled=True)
    return numerator * lax.rsqrt(total_square / K + EPS)[:, None] * K ** (-0.5)


def solution(mesh):
    return jax.shard_map(
        local,
        mesh=mesh,
        in_specs=(
            P("dp", None, "mp"),
            P("dp", None, "mp"),
            P("dp", None, None),
            P("dp", None, None),
            P("dp", None, "mp"),
            P("dp", None),
            P("mp", None),
            P(None, "mp"),
            P("mp", None),
            P(),
            P(None, "mp"),
            P(None, "mp"),
            P(),
            P(),
            P(),
            P("dp", "mp"),
        ),
        out_specs=P("dp", "mp"),
        check_vma=False,
    )
```

profile of v0, /device:TPU:2, one launch (start us, length us, event | category | flops | bytes accessed | tf_op | source)
XLA Modules:
  0.0 423.8 jit_solution(10338486193786208510)
XLA Ops:
  7.5 1.1 constant_dynamic-slice_fusion
  8.7 2.5 fusion.22
  11.2 0.4 compare_and_fusion
  11.7 6.1 %fusion.55 = (f32[2,4,512]{2,1,0:T(4,128)S(1)}, f32[2,4,512,512]{2,3,1,0:T(8,128)}) fusion(f32[2,4,512,512]{3,2,1,0:T(8,128)S(1)} %fusion.22, pred[2,512,512]{1,2,0:T(8,128)(4,1)S(1)} %compare_and_fusion), kind=kOutput, calls=%fused_computation.71 | output fusion | flops 12583423 | bytes 17317888 | tf_op jit(solution)/shard_map/sub | solution.py:74
  17.8 4.8 %convert_reduce_fusion = bf16[2,512,128]{2,1,0:T(8,128)(2,1)S(1)} fusion(f32[2,4,512,512]{2,3,1,0:T(8,128)} %get-tuple-element.10, f32[2,4,512]{2,1,0:T(4,128)S(1)} %get-tuple-element.9, bf16[2,512,512]{2,1,0:T(8,128)(2,1)S(1)} %copy-done), kind=kOutput, calls=%fused_computation.18 | convolution fusion | flops 542507008 | bytes 9715712 | tf_op jit(solution)/shard_map/bhqk,bqhd->bkhd/dot_general | solution.py:76
  22.6 1.0 copy-done.9
  23.5 1.5 fusion.1
  25.1 1.6 multiply_convert_fusion
  26.7 0.3 fusion.44
  27.0 1.0 fusion.46
  28.0 1.1 pad_maximum_fusion
  29.1 1.0 copy.37
  30.1 1.7 copy.38
  31.7 2.4 convolution_bitcast_fusion
  34.2 89.1 %all-reduce.2 = (bf16[2,512,256]{1,2,0:T(8,128)(2,1)}, bf16[2,512,256]{1,2,0:T(8,128)(2,1)}) all-reduce(f32[2,512,256]{1,2,0:T(8,128)} %convolution_bitcast_fusion, f32[2,512,256]{1,2,0:T(8,128)} %pad_maximum_fusion), channel_id=1, replica_groups=mesh['dp'=32,'mp'=16] {'mp'}, use_global_device_ids=true, to_apply=%region_5.6 | all-reduce | flops 524288 | bytes 3145728 | tf_op jit(solution)/shard_map/psum | solution.py:99
  123.2 1.4 fusion.39
  124.7 1.2 fusion.37
  125.9 1.5 convolution_bitcast_fusion.1
  127.5 1.3 maximum_bitcast_fusion
  128.8 3.2 copy.44
  132.0 0.8 dynamic-slice_add_fusion
  133.0 60.1 %scatter_fusion = f32[512,2,128]{2,1,0:T(2,128)S(1)} fusion(f32[512,2,128]{2,1,0:T(2,128)S(1)} %broadcast_in_dim.12, s32[1664]{0:T(1024)S(1)} %pad_add_fusion, f32[1664,2,128]{2,1,0:T(2,128)S(1)} %copy.44), kind=kCustom, calls=%fused_computation | custom fusion | flops 425984 | bytes 5118464 | tf_op jit(solution)/shard_map/scatter-add | solution.py:119
  193.1 0.5 fusion.18
  193.6 1.9 copy.58
  195.6 0.5 all-gather.2.cloned.1.call-update
  196.1 92.7 %reduce-scatter.7.cloned.1.call-done = bf16[512,2]{1,0:T(8,128)(2,1)} async-done(((bf16[8192,2]{1,0:T(8,128)(2,1)}), bf16[512,2]{1,0:T(8,128)(2,1)}) %reduce-scatter.7.cloned.1.call-update) | async-done | bytes 2064
  288.8 1.0 copy.55
  289.9 33.3 %psum.23 = f32[2]{0:T(128)S(1)} all-reduce(f32[2]{0:T(128)S(1)} %multiply_reduce_fusion), channel_id=1, replica_groups=mesh['dp'=32,'mp'=16] {'mp'}, use_global_device_ids=true, to_apply=%region_10.11 | all-reduce | flops 2 | bytes 16 | tf_op jit(solution)/shard_map/psum | solution.py:142
  323.2 2.5 convolution_bitcast_fusion.2
  325.8 89.1 %reduce-scatter.9.cloned.1.call-done = f32[64,2]{1,0:T(8,128)} async-done(((f32[1024,2]{1,0:T(8,128)}), f32[64,2]{1,0:T(8,128)}) %reduce-scatter.9.cloned.1.call-update) | async-done | bytes 528
  414.9 0.8 copy.57
  415.7 0.6 multiply_multiply_fusion
  (34 shorter events, 0.8 us)
Async XLA Ops:
  7.4 10.4 %copy-start = (bf16[2,512,512]{2,1,0:T(8,128)(2,1)S(1)}, bf16[2,512,512]{2,1,0:T(8,128)(2,1)}, u32[]{:S(2)}) copy-start(bf16[2,512,512]{2,1,0:T(8,128)(2,1)} %param.20) | copy-start | bytes 3145732
  7.4 3.9 copy-start.6
  7.4 281.4 %reduce-scatter.7.cloned.1.call-start = ((), (), s32[]{:S(2)}) async-start(), calls=%async_computation.3 | async-start | bytes 2228224
  17.8 5.8 %copy-start.9 = (f32[2,4,512,512]{2,3,1,0:T(8,128)S(1)}, f32[2,4,512,512]{2,3,1,0:T(8,128)}, u32[]{:S(2)}) copy-start(f32[2,4,512,512]{2,3,1,0:T(8,128)} %get-tuple-element.10) | copy-start | bytes 25165828
  22.6 4.4 %copy-start.2 = (bf16[2,512,128]{2,1,0:T(8,128)(2,1)}, bf16[2,512,128]{2,1,0:T(8,128)(2,1)S(1)}, u32[]{:S(2)}) copy-start(bf16[2,512,128]{2,1,0:T(8,128)(2,1)S(1)} %convert_reduce_fusion) | copy-start | bytes 786436
  25.0 1.6 copy-start.5
  25.1 6.7 %copy-start.1 = (bf16[2,512,512]{2,1,0:T(8,128)(2,1)S(1)}, bf16[2,512,512]{2,1,0:T(8,128)(2,1)}, u32[]{:S(2)}) copy-start(bf16[2,512,512]{2,1,0:T(8,128)(2,1)} %param.16) | copy-start | bytes 3145732
  28.0 96.7 %copy-start.3 = (bf16[2,512,128]{2,1,0:T(8,128)(2,1)S(1)}, bf16[2,512,128]{2,1,0:T(8,128)(2,1)}, u32[]{:S(2)}) copy-start(bf16[2,512,128]{2,1,0:T(8,128)(2,1)} %copy-done.2) | copy-start | bytes 786436
  34.1 97.9 %copy-start.7 = (s32[3,512]{1,0:T(4,128)S(1)}, s32[3,512]{1,0:T(4,128)}, u32[]{:S(2)}) copy-start(s32[3,512]{1,0:T(4,128)} %param.27) | copy-start | bytes 18436
  34.2 97.9 %copy-start.8 = (s32[3,512]{1,0:T(4,128)S(1)}, s32[3,512]{1,0:T(4,128)}, u32[]{:S(2)}) copy-start(s32[3,512]{1,0:T(4,128)} %param.26) | copy-start | bytes 18436
  125.8 67.2 %copy-start.4 = (bf16[8,128,128]{2,1,0:T(8,128)(2,1)S(1)}, bf16[8,128,128]{2,1,0:T(8,128)(2,1)}, u32[]{:S(2)}) copy-start(bf16[8,128,128]{2,1,0:T(8,128)(2,1)} %param.30) | copy-start | bytes 786436
  195.5 127.7 %all-gather.2.cloned.1.call-start = ((), (), s32[]{:S(2)}) async-start(), calls=%async_computation.2 | async-start | bytes 1081344 | tf_op jit(solution)/shard_map/all_gather | solution.py:139
  196.1 218.8 %reduce-scatter.9.cloned.1.call-start = ((), (), s32[]{:S(2)}) async-start(), calls=%async_computation.4 | async-start | bytes 557056
Sparse Core Ops, SparseCore 0:
  195.6 93.1 reduce-scatter.6
  325.9 88.9 reduce-scatter.8
Sparse Core Ops, SparseCore 1:
  198.3 74.8 all-gather.1
where the time goes:
time: 424 us
  waiting for transfers between devices  182 us (43%)
  blocking collectives  122 us (29%)
  other arithmetic  70.6 us (17%)
  matrix products  21.2 us (5%)
  between operations  15.1 us (4%)
  local copies, waits for them, and re-layouts  12.1 us (3%)
    unnamed x5, waiting for transfers between devices  182 us
    psum x1, blocking collectives, local(): lowrank_in, lowrank_back = lax.psum((lowrank_part, back_part), 'mp')  89.1 us
    scatter-add x1, other arithmetic, local(): jax.ops.segment_sum(jnp.moveaxis(grad_rows, 1, 0), bucket_ids, num_segmen...  60.1 us
    psum x1, blocking collectives, local(): total_square = lax.psum(feat_square, 'mp')  33.3 us
  transfers between devices with their start and end apart: 3, of which 2 were waited for; matrix products, arithmetic and copies ran while one was open for 0% of the time, Pallas kernels for 0%

commit v1 on v0

--- a/solution.py
+++ b/solution.py
@@ -3,6 +3,7 @@
 import jax.numpy as jnp
 from jax import lax
 from jax.sharding import PartitionSpec as P
+from jax.lax import all_gather
 
 H = 64
 KVH = 8
@@ -139,7 +140,8 @@
         lax.all_gather(seed_feats, "dp", axis=0, tiled=True),
         preferred_element_type=jnp.float32,
     )
-    total_square = lax.psum(feat_square, "mp")
+    k_now = all_gather(feat_square, axis_name="mp")
+    total_square = jnp.sum(k_now, axis=0)
     numerator = lax.psum_scatter(partial_value, "mp", scatter_dimension=1, tiled=True)
     return numerator * lax.rsqrt(total_square / K + EPS)[:, None] * K ** (-0.5)
 

time: 424 us -> 425 us (level)
    psum x1 -> x0, blocking collectives: 33.3 us -> none  [local(): total_square = lax.psum(feat_square, 'mp')]
    unnamed x0 -> x1, blocking collectives: none -> 33.2 us
    unnamed x25 -> x28, local copies, waits for them, and re-layouts: 7.41 us -> 8.92 us
  transfers between devices with their start and end apart: 3 -> 3, of which waited for: 2 -> 2; matrix products, arithmetic and copies ran while one was open for 0% -> 1% of each run, Pallas kernels for 0% -> 0%
where the time goes in v1:
time: 425 us; the launch traced here: 424 us
  waiting for transfers between devices  180 us (42%)
  blocking collectives  122 us (29%)
  other arithmetic  70.6 us (17%)
  matrix products  21.2 us (5%)
  between operations  15.8 us (4%)
  local copies, waits for them, and re-layouts  13.7 us (3%)
    unnamed x5, waiting for transfers between devices  180 us
    psum x1, blocking collectives, local(): lowrank_in, lowrank_back = lax.psum((lowrank_part, back_part), 'mp')  89.1 us
    scatter-add x1, other arithmetic, local(): jax.ops.segment_sum(jnp.moveaxis(grad_rows, 1, 0), bucket_ids, num_segmen...  60.1 us
    unnamed x1, blocking collectives  33.2 us
    unnamed x28, local copies, waits for them, and re-layouts  8.92 us
  transfers between devices with their start and end apart: 3, of which 2 were waited for; matrix products, arithmetic and copies ran while one was open for 1% of the time, Pallas kernels for 0%

profile of v1, /device:TPU:2, one launch (start us, length us, event | category | flops | bytes accessed | tf_op | source)
XLA Modules:
  0.0 424.2 jit_solution(3363113316999388174)
XLA Ops:
  7.5 1.1 constant_dynamic-slice_fusion
  8.7 2.5 fusion.22
  11.2 0.4 compare_and_fusion
  11.7 6.1 %fusion.55 = (f32[2,4,512]{2,1,0:T(4,128)S(1)}, f32[2,4,512,512]{2,3,1,0:T(8,128)}) fusion(f32[2,4,512,512]{3,2,1,0:T(8,128)S(1)} %fusion.22, pred[2,512,512]{1,2,0:T(8,128)(4,1)S(1)} %compare_and_fusion), kind=kOutput, calls=%fused_computation.71 | output fusion | flops 12583423 | bytes 17317888 | tf_op jit(solution)/shard_map/sub | solution.py:75
  17.8 4.8 %convert_reduce_fusion = bf16[2,512,128]{2,1,0:T(8,128)(2,1)S(1)} fusion(f32[2,4,512,512]{2,3,1,0:T(8,128)} %get-tuple-element.10, f32[2,4,512]{2,1,0:T(4,128)S(1)} %get-tuple-element.9, bf16[2,512,512]{2,1,0:T(8,128)(2,1)S(1)} %copy-done), kind=kOutput, calls=%fused_computation.18 | convolution fusion | flops 542507008 | bytes 9715712 | tf_op jit(solution)/shard_map/bhqk,bqhd->bkhd/dot_general | solution.py:77
  22.6 1.0 copy-done.9
  23.5 1.5 fusion.1
  25.1 1.6 multiply_convert_fusion
  27.0 1.0 fusion.46
  28.0 1.1 pad_maximum_fusion
  29.1 1.0 copy.52
  30.1 1.7 copy.53
  31.7 2.4 convolution_bitcast_fusion
  34.2 89.1 %all-reduce.3 = (bf16[2,512,256]{1,2,0:T(8,128)(2,1)}, bf16[2,512,256]{1,2,0:T(8,128)(2,1)}) all-reduce(f32[2,512,256]{1,2,0:T(8,128)} %convolution_bitcast_fusion, f32[2,512,256]{1,2,0:T(8,128)} %pad_maximum_fusion), channel_id=1, replica_groups=mesh['dp'=32,'mp'=16] {'mp'}, use_global_device_ids=true, to_apply=%region_5.6 | all-reduce | flops 524288 | bytes 3145728 | tf_op jit(solution)/shard_map/psum | solution.py:100
  123.2 1.4 fusion.39
  124.7 1.2 fusion.37
  125.9 1.5 convolution_bitcast_fusion.1
  127.5 1.3 maximum_bitcast_fusion
  128.8 3.2 copy.59
  132.0 0.8 dynamic-slice_add_fusion
  133.0 60.1 %scatter_fusion = f32[512,2,128]{2,1,0:T(2,128)S(1)} fusion(f32[512,2,128]{2,1,0:T(2,128)S(1)} %broadcast_in_dim.12, s32[1664]{0:T(1024)S(1)} %pad_add_fusion, f32[1664,2,128]{2,1,0:T(2,128)S(1)} %copy.59), kind=kCustom, calls=%fused_computation | custom fusion | flops 425984 | bytes 5118464 | tf_op jit(solution)/shard_map/scatter-add | solution.py:120
  193.1 0.5 fusion.18
  193.6 1.9 copy.74
  195.6 0.5 all-gather.3.cloned.1.call-update
  196.1 1.3 dynamic-slice
  198.1 90.7 %reduce-scatter.7.cloned.1.call-done = bf16[512,2]{1,0:T(8,128)(2,1)} async-done(((bf16[8192,2]{1,0:T(8,128)(2,1)}), bf16[512,2]{1,0:T(8,128)(2,1)}) %reduce-scatter.7.cloned.1.call-update) | async-done | bytes 2064
  288.8 1.0 copy.71
  290.2 33.2 %all-reduce = f32[32]{0:T(128)S(1)} all-reduce(f32[32]{0:T(128)S(1)} %dynamic-update-slice), channel_id=2, replica_groups=mesh['dp'=32,'mp'=16] {'mp'}, use_global_device_ids=true, to_apply=%add | all-reduce | flops 32 | bytes 256
  323.6 2.5 convolution_bitcast_fusion.2
  326.1 89.1 %reduce-scatter.9.cloned.1.call-done = f32[64,2]{1,0:T(8,128)} async-done(((f32[1024,2]{1,0:T(8,128)}), f32[64,2]{1,0:T(8,128)}) %reduce-scatter.9.cloned.1.call-update) | async-done | bytes 528
  415.3 0.8 copy.73
  416.1 0.6 multiply_multiply_fusion
  (39 shorter events, 1.4 us)
Async XLA Ops:
  7.4 10.4 %copy-start = (bf16[2,512,512]{2,1,0:T(8,128)(2,1)S(1)}, bf16[2,512,512]{2,1,0:T(8,128)(2,1)}, u32[]{:S(2)}) copy-start(bf16[2,512,512]{2,1,0:T(8,128)(2,1)} %param.20) | copy-start | bytes 3145732
  7.4 3.9 copy-start.6
  7.4 281.4 %reduce-scatter.7.cloned.1.call-start = ((), (), s32[]{:S(2)}) async-start(), calls=%async_computation.3 | async-start | bytes 2228224
  17.8 5.8 %copy-start.9 = (f32[2,4,512,512]{2,3,1,0:T(8,128)S(1)}, f32[2,4,512,512]{2,3,1,0:T(8,128)}, u32[]{:S(2)}) copy-start(f32[2,4,512,512]{2,3,1,0:T(8,128)} %get-tuple-element.10) | copy-start | bytes 25165828
  22.6 4.4 %copy-start.2 = (bf16[2,512,128]{2,1,0:T(8,128)(2,1)}, bf16[2,512,128]{2,1,0:T(8,128)(2,1)S(1)}, u32[]{:S(2)}) copy-start(bf16[2,512,128]{2,1,0:T(8,128)(2,1)S(1)} %convert_reduce_fusion) | copy-start | bytes 786436
  25.0 1.6 copy-start.5
  25.1 6.7 %copy-start.1 = (bf16[2,512,512]{2,1,0:T(8,128)(2,1)S(1)}, bf16[2,512,512]{2,1,0:T(8,128)(2,1)}, u32[]{:S(2)}) copy-start(bf16[2,512,512]{2,1,0:T(8,128)(2,1)} %param.16) | copy-start | bytes 3145732
  28.0 96.7 %copy-start.3 = (bf16[2,512,128]{2,1,0:T(8,128)(2,1)S(1)}, bf16[2,512,128]{2,1,0:T(8,128)(2,1)}, u32[]{:S(2)}) copy-start(bf16[2,512,128]{2,1,0:T(8,128)(2,1)} %copy-done.2) | copy-start | bytes 786436
  34.1 97.9 %copy-start.7 = (s32[3,512]{1,0:T(4,128)S(1)}, s32[3,512]{1,0:T(4,128)}, u32[]{:S(2)}) copy-start(s32[3,512]{1,0:T(4,128)} %param.27) | copy-start | bytes 18436
  34.2 97.9 %copy-start.8 = (s32[3,512]{1,0:T(4,128)S(1)}, s32[3,512]{1,0:T(4,128)}, u32[]{:S(2)}) copy-start(s32[3,512]{1,0:T(4,128)} %param.26) | copy-start | bytes 18436
  125.8 67.2 %copy-start.4 = (bf16[8,128,128]{2,1,0:T(8,128)(2,1)S(1)}, bf16[8,128,128]{2,1,0:T(8,128)(2,1)}, u32[]{:S(2)}) copy-start(bf16[8,128,128]{2,1,0:T(8,128)(2,1)} %param.30) | copy-start | bytes 786436
  195.5 128.0 %all-gather.3.cloned.1.call-start = ((), (), s32[]{:S(2)}) async-start(), calls=%async_computation.2 | async-start | bytes 1081344 | tf_op jit(solution)/shard_map/all_gather | solution.py:140
  196.1 219.2 %reduce-scatter.9.cloned.1.call-start = ((), (), s32[]{:S(2)}) async-start(), calls=%async_computation.4 | async-start | bytes 557056
Sparse Core Ops, SparseCore 0:
  195.6 93.1 reduce-scatter.6
  326.2 88.9 reduce-scatter.8
Sparse Core Ops, SparseCore 1:
  198.3 74.8 all-gather.2
